TPU v7x, 32 devices: a whole 2x2x4 slice. The times are simulated.
32 devices in a mesh: front: 8 (over y, x, core), tile: 4 (over z).
Axes of the slice: x: 2, y: 2, z: 4, core: 2. Of those that a mesh axis runs over, the one named last changes fastest.
Arguments:
- pivot_inverse: float32 [8, 2, 512, 512], P('front', None, 'tile'), may hold values from -0.26516504 to 0.26516504
- panel_upper: float32 [8, 2, 512, 2048], P('front', None, None, 'tile'), may hold values from -6 to 6
- panel_lower: float32 [8, 2, 2048, 512], P('front', None, 'tile'), may hold values from -4.2426407 to 4.2426407
- index_map: int32 [8, 2, 2048], replicated, may hold values from 0 to 4095, as said below
- parent_base: float32 [8, 4096, 4096], P('front', None, 'tile'), may hold values from -512 to 512
Outputs:
- parent_front: float32 [8, 4096, 4096], P('front', None, 'tile')
Inputs may be any that keep to these rules, and one draw needn't show every extreme that they name: Each list index_map[g, c] holds 2048 distinct parent indices in no particular order, among them 0 and 4095.
All inputs are finite; a program needn't handle non-finite values.
Results may differ from a plain program's by a relative error of at most 0.0003.
Values sent between devices are 32-bit elements; how exact they have to be, the bound alone decides.
A program may use at most 128 MiB of HBM per device.

v0:
```python
import jax
import jax.numpy as jnp
from jax import lax
from jax.sharding import PartitionSpec as P


def partner_2(value, axis, distance):
    mask = 2**distance
    pairs = [(source, source ^ mask) for source in range(lax.axis_size(axis))]
    return lax.ppermute(value, axis, pairs)


def split_parts(matrix):
    high = matrix.astype(jnp.bfloat16)
    back = lax.optimization_barrier(high).astype(jnp.float32)
    low = (matrix - back).astype(jnp.bfloat16)
    return (high, low)


def split_product(left, right):
    left_high, left_low = split_parts(left)
    right_high, right_low = split_parts(right)
    total = jnp.dot(left_high, right_high, preferred_element_type=jnp.float32)
    total = total + jnp.dot(left_high, right_low, preferred_element_type=jnp.float32)
    return total + jnp.dot(left_low, right_high, preferred_element_type=jnp.float32)


def contribution(inverse_rows, upper_cols, lower_rows, mapping, parent_order, col_start, width):
    factor_local = split_product(
        lax.all_gather(inverse_rows, "tile", axis=0, tiled=True), upper_cols
    )
    factor_full = lax.all_gather(factor_local, "tile", axis=1, tiled=True)
    count = mapping.shape[0]
    inverse_map = (
        jnp.full((parent_order,), -1, jnp.int32).at[mapping].set(jnp.arange(count, dtype=jnp.int32))
    )
    own_cols = lax.dynamic_slice_in_dim(inverse_map, col_start, width)
    picked = jnp.take(factor_full, jnp.clip(own_cols, 0, count - 1), axis=1)
    factor_ext = jnp.where(own_cols[None, :] >= 0, picked, 0.0)
    update = split_product(lax.all_gather(lower_rows, "tile", axis=0, tiled=True), factor_ext)
    placed = jnp.take(update, jnp.clip(inverse_map, 0, count - 1), axis=0)
    return jnp.where(inverse_map[:, None] >= 0, placed, 0.0)


def shards(pivot_inverse, panel_upper, panel_lower, index_map, parent_base):
    base = parent_base[0]
    parent_order = base.shape[0]
    width = base.shape[1]
    col_start = lax.axis_index("tile") * width
    group = lax.axis_index("front")
    partner = jnp.bitwise_xor(group, 1)
    own_lists = lax.dynamic_index_in_dim(index_map, group, 0, keepdims=False)
    first = contribution(
        pivot_inverse[0, 0],
        panel_upper[0, 0],
        panel_lower[0, 0],
        own_lists[0],
        parent_order,
        col_start,
        width,
    )
    inverse_far, upper_far, lower_far = partner_2(
        (pivot_inverse[0, 1], panel_upper[0, 1], panel_lower[0, 1]), "front", 0
    )
    far_lists = lax.dynamic_index_in_dim(index_map, partner, 0, keepdims=False)
    second = contribution(
        inverse_far, upper_far, lower_far, far_lists[1], parent_order, col_start, width
    )
    result = base - first - second
    return result[None]


def solution(mesh):
    return jax.shard_map(
        shards,
        mesh=mesh,
        in_specs=(
            P("front", None, "tile", None),
            P("front", None, None, "tile"),
            P("front", None, "tile", None),
            P(),
            P("front", None, "tile"),
        ),
        out_specs=P("front", None, "tile"),
        check_vma=False,
    )
```

profile of v0, /device:TPU:0, one launch (start us, length us, event | category | flops | bytes accessed | tf_op | source)
XLA Modules:
  0.0 489.1 jit_solution(886171841791117175)
XLA Ops:
  6.5 1.9 fusion.39
  8.5 0.6 collective-permute-start
  9.1 1.2 collective-permute-done
  10.3 0.7 copy-done.7
  11.0 3.0 fusion.38
  14.2 0.4 collective-permute-start.2
  14.6 2.5 collective-permute-done.2
  17.1 1.0 copy-done.6
  18.2 0.1 bitcast_convert_fusion.1
  18.2 21.4 %all-gather.17.cloned.1.call-done = f32[1,1,512,512]{3,2,1,0:T(8,128)} async-done(((f32[1,1,128,512]{3,2,1,0:T(8,128)}), f32[1,1,512,512]{3,2,1,0:T(8,128)}) %all-gather.17.cloned.1.call-update) | async-done | bytes 1048592 | tf_op jit(solution)/shard_map/all_gather | solution.py:30
  39.6 1.4 bitcast_convert_fusion.2
  41.0 0.4 fusion.40
  41.5 0.4 fusion.23
  41.9 1.4 fusion.8
  43.4 0.1 slice_bitcast_fusion.1
  43.5 0.1 collective-permute-start.1
  43.6 2.6 collective-permute-done.1
  46.3 22.3 %all-gather.11.cloned.1.call-done = f32[512,512]{1,0:T(8,128)} async-done(((f32[128,512]{1,0:T(8,128)}), f32[512,512]{1,0:T(8,128)}) %all-gather.11.cloned.1.call-update) | async-done | bytes 1048592 | tf_op jit(solution)/shard_map/all_gather | solution.py:30
  68.6 1.3 convert_element_type.84
  69.9 1.7 fusion.22
  71.6 0.5 convolution_bitcast_fusion
  72.0 1.4 fusion.9
  73.5 0.8 compare_select_fusion.1
  74.3 8.1 %scatter_custom_fusion = s32[4096]{0:T(1024)S(1)} fusion(s32[2048]{0:T(1024)S(1)} %bitcast.87, s32[2048]{0:T(1024)S(1)} %iota.6, s32[]{:T(128)} %constant.10.clone.1), kind=kCustom, calls=%fused_computation.69 | custom fusion | bytes 16388 | tf_op jit(solution)/shard_map/scatter | solution.py:35
  82.3 8.2 %scatter_custom_fusion.1 = s32[4096]{0:T(1024)S(1)} fusion(s32[2048]{0:T(1024)S(1)} %bitcast.86, s32[2048]{0:T(1024)S(1)} %iota.7, s32[]{:T(128)} %constant.10.clone.1), kind=kCustom, calls=%fused_computation.67 | custom fusion | bytes 16388 | tf_op jit(solution)/shard_map/scatter | solution.py:35
  90.7 59.6 %all-gather.19.cloned.1.call-done = f32[1,1,2048,512]{3,2,1,0:T(8,128)} async-done(((f32[1,1,512,512]{3,2,1,0:T(8,128)}), f32[1,1,2048,512]{3,2,1,0:T(8,128)}) %all-gather.19.cloned.1.call-update) | async-done | bytes 4194320 | tf_op jit(solution)/shard_map/all_gather | solution.py:40
  150.3 3.8 bitcast_convert_fusion
  154.2 76.9 %all-gather.15.cloned.1.call-done = f32[2048,512]{1,0:T(8,128)} async-done(((f32[512,512]{1,0:T(8,128)}), f32[2048,512]{1,0:T(8,128)}) %all-gather.15.cloned.1.call-update) | async-done | bytes 4194320 | tf_op jit(solution)/shard_map/all_gather | solution.py:40
  231.0 3.7 convert_element_type.91
  234.8 76.9 %all-gather.9.cloned.1.call-done = f32[512,2048]{1,0:T(8,128)} async-done(((f32[512,512]{1,0:T(8,128)}), f32[512,2048]{1,0:T(8,128)}) %all-gather.9.cloned.1.call-update) | async-done | bytes 4194320 | tf_op jit(solution)/shard_map/all_gather | solution.py:32
  311.7 5.3 %copy.15 = f32[512,2048]{0,1:T(8,128)} copy(f32[512,2048]{1,0:T(8,128)} %all-gather.9.cloned.1.call-done) | data formatting | bytes 8388608 | tf_op jit(solution)/shard_map/all_gather | solution.py:32
  317.0 6.6 %gather_fusion = f32[1024,512]{1,0:T(8,128)S(1)} fusion(f32[512,2048]{0,1:T(8,128)} %copy.15, s32[1024]{0:T(1024)S(1)} %fusion.32), kind=kCustom, calls=%fused_computation.clone | custom fusion | bytes 4198400 | tf_op jit(solution)/shard_map/jit(_take)/gather | solution.py:38
  323.6 0.8 fusion.5
  324.5 7.5 %fusion.41 = f32[1024,2048]{1,0:T(8,128)} fusion(bf16[512,1024]{0,1:T(8,128)(2,1)S(1)} %fusion.5, bf16[2048,512]{1,0:T(8,128)(2,1)} %bitcast_convert_fusion), kind=kOutput, calls=%fused_computation.84 | convolution fusion | flops 2147483648 | bytes 11534336 | tf_op jit(solution)/shard_map/dot_general | solution.py:23
  332.0 2.5 fusion.10
  334.5 9.5 %bitcast_add_fusion.1 = f32[2048,1024]{0,1:T(8,128)} fusion(f32[1024,2048]{1,0:T(8,128)} %fusion.41, f32[1024,2048]{1,0:T(8,128)S(1)} %fusion.10, bf16[512,1024]{0,1:T(8,128)(2,1)S(1)} %fusion.5, f32[1,1,2048,512]{3,2,1,0:T(8,128)S(1)} %copy-done.3, bf16[2048,512]{1,0:T(8,128)(2,1)S(1)} %copy-done.1), kind=kOutput, calls=%fused_computation.12 | convolution fusion | flops 2154823680 | bytes 32505856 | tf_op jit(solution)/shard_map/dot_general | solution.py:25
  343.9 9.4 %copy.17 = f32[2048,1024]{1,0:T(8,128)} copy(f32[2048,1024]{0,1:T(8,128)} %bitcast_add_fusion.1) | data formatting | bytes 16777216 | tf_op jit(solution)/shard_map/add | solution.py:25
  353.3 25.9 %gather_fusion.1 = f32[4096,1024]{1,0:T(8,128)} fusion(f32[2048,1024]{1,0:T(8,128)} %copy.17, s32[4096]{0:T(1024)S(1)} %fusion.26), kind=kCustom, calls=%fused_computation.1.clone | custom fusion | bytes 33570816 | tf_op jit(solution)/shard_map/jit(_take)/gather | solution.py:41
  379.2 13.2 %all-gather.13.cloned.1.call-done = f32[512,2048]{1,0:T(8,128)} async-done(((f32[512,512]{1,0:T(8,128)}), f32[512,2048]{1,0:T(8,128)}) %all-gather.13.cloned.1.call-update) | async-done | bytes 4194320 | tf_op jit(solution)/shard_map/all_gather | solution.py:32
  392.4 5.3 %copy.19 = f32[512,2048]{0,1:T(8,128)} copy(f32[512,2048]{1,0:T(8,128)} %all-gather.13.cloned.1.call-done) | data formatting | bytes 8388608 | tf_op jit(solution)/shard_map/all_gather | solution.py:32
  397.7 6.2 %gather_fusion.2 = f32[1024,512]{1,0:T(8,128)S(1)} fusion(f32[512,2048]{0,1:T(8,128)} %copy.19, s32[1024]{0:T(1024)S(1)} %fusion.33), kind=kCustom, calls=%fused_computation.2.clone | custom fusion | bytes 4198400 | tf_op jit(solution)/shard_map/jit(_take)/gather | solution.py:38
  403.9 1.1 fusion.6
  405.0 7.5 %fusion.42 = f32[1024,2048]{1,0:T(8,128)} fusion(bf16[512,1024]{0,1:T(8,128)(2,1)S(1)} %fusion.6, bf16[2048,512]{1,0:T(8,128)(2,1)} %convert_element_type.91), kind=kOutput, calls=%fused_computation.85 | convolution fusion | flops 2147483648 | bytes 11534336 | tf_op jit(solution)/shard_map/dot_general | solution.py:23
  412.5 2.5 fusion.11
  415.0 9.4 %bitcast_add_fusion = f32[2048,1024]{0,1:T(8,128)} fusion(f32[1024,2048]{1,0:T(8,128)} %fusion.42, f32[1024,2048]{1,0:T(8,128)S(1)} %fusion.11, bf16[512,1024]{0,1:T(8,128)(2,1)S(1)} %fusion.6, f32[2048,512]{1,0:T(8,128)S(1)} %copy-done.2, bf16[2048,512]{1,0:T(8,128)(2,1)S(1)} %copy-done), kind=kOutput, calls=%fused_computation.11 | convolution fusion | flops 2154823680 | bytes 32505856 | tf_op jit(solution)/shard_map/dot_general | solution.py:25
  424.4 9.3 %copy.21 = f32[2048,1024]{1,0:T(8,128)} copy(f32[2048,1024]{0,1:T(8,128)} %bitcast_add_fusion) | data formatting | bytes 16777216 | tf_op jit(solution)/shard_map/add | solution.py:25
  433.7 25.5 %gather_fusion.3 = f32[4096,1024]{1,0:T(8,128)} fusion(f32[2048,1024]{1,0:T(8,128)} %copy.21, s32[4096]{0:T(1024)S(1)} %fusion.27), kind=kCustom, calls=%fused_computation.3.clone | custom fusion | bytes 33570816 | tf_op jit(solution)/shard_map/jit(_take)/gather | solution.py:41
  459.2 23.0 %fusion.1 = f32[1,4096,1024]{2,1,0:T(8,128)} fusion(f32[1,4096,1024]{2,1,0:T(8,128)} %param.13, f32[4096,1024]{1,0:T(8,128)} %gather_fusion.3, f32[4096,1024]{1,0:T(8,128)} %gather_fusion.1, pred[4096]{0:T(1024)(128)(4,1)S(1)} %get-tuple-element.16, pred[4096]{0:T(1024)(128)(4,1)S(1)} %get-tuple-element.21, pred[4096]{0:T(1024)(128)(4,1)S(1)} %get-tuple-element.15, ...), kind=kLoop, calls=%fused_computation.8 | loop fusion | flops 25165824 | bytes 67125248 | tf_op jit(solution)/shard_map/broadcast_in_dim | solution.py:70
  (36 shorter events, 0.5 us)
Async XLA Ops:
  6.5 11.6 %copy-start.4 = (f32[1,2,512,512]{3,2,1,0:T(8,128)S(1)}, f32[1,2,512,512]{3,2,1,0:T(8,128)}, u32[]{:S(2)}) copy-start(f32[1,2,512,512]{3,2,1,0:T(8,128)} %param.10) | copy-start | bytes 6291460
  6.5 33.1 %all-gather.17.cloned.1.call-start = ((), (), s32[]{:S(2)}) async-start(), calls=%async_computation.4 | async-start | bytes 1310720 | tf_op jit(solution)/shard_map/all_gather | solution.py:30
  8.5 60.1 %all-gather.11.cloned.1.call-start = ((), (), s32[]{:S(2)}) async-start(), calls=%async_computation.1 | async-start | bytes 1310720 | tf_op jit(solution)/shard_map/all_gather | solution.py:30
  8.5 1.7 collective-permute-start
  10.3 0.7 copy-start.7
  11.0 139.3 %all-gather.19.cloned.1.call-start = ((), (), s32[]{:S(2)}) async-start(), calls=%async_computation.5 | async-start | bytes 5242880 | tf_op jit(solution)/shard_map/all_gather | solution.py:40
  14.1 216.9 %all-gather.15.cloned.1.call-start = ((), (), s32[]{:S(2)}) async-start(), calls=%async_computation.3 | async-start | bytes 5242880 | tf_op jit(solution)/shard_map/all_gather | solution.py:40
  14.2 2.9 collective-permute-start.2
  17.1 1.0 copy-start.6
  18.1 293.6 %all-gather.9.cloned.1.call-start = ((), (), s32[]{:S(2)}) async-start(), calls=%async_computation | async-start | bytes 5242880 | tf_op jit(solution)/shard_map/all_gather | solution.py:32
  39.6 1.8 copy-start.5
  43.4 349.0 %all-gather.13.cloned.1.call-start = ((), (), s32[]{:S(2)}) async-start(), calls=%async_computation.2 | async-start | bytes 5242880 | tf_op jit(solution)/shard_map/all_gather | solution.py:32
  43.5 2.7 collective-permute-start.1
  324.5 7.5 %copy-start.1 = (bf16[2048,512]{1,0:T(8,128)(2,1)S(1)}, bf16[2048,512]{1,0:T(8,128)(2,1)}, u32[]{:S(2)}) copy-start(bf16[2048,512]{1,0:T(8,128)(2,1)} %bitcast_convert_fusion) | copy-start | bytes 6291460
  332.0 2.5 copy-start.3
  405.0 7.5 %copy-start = (bf16[2048,512]{1,0:T(8,128)(2,1)S(1)}, bf16[2048,512]{1,0:T(8,128)(2,1)}, u32[]{:S(2)}) copy-start(bf16[2048,512]{1,0:T(8,128)(2,1)} %convert_element_type.91) | copy-start | bytes 6291460
  412.5 2.5 copy-start.2
Sparse Core Ops, SparseCore 0:
  8.9 30.6 all-gather.16
  41.2 27.3 all-gather.10
  70.2 80.1 all-gather.18
  151.7 79.2 all-gather.14
  232.4 79.2 all-gather.8
  313.1 79.2 all-gather.12
where the time goes:
time: 490 us; the launch traced here: 489 us
  waiting for transfers between devices  277 us (57%)
  local copies, waits for them, and re-layouts  117 us (24%)
  matrix products  44.7 us (9%)
  other arithmetic  36.1 us (7%)
  between operations  13.7 us (3%)
    all_gather x2, waiting for transfers between devices, contribution(): lax.all_gather(lower_rows, 'tile', axis=0, tiled=True)  136 us
    all_gather x2, waiting for transfers between devices, contribution(): factor_full = lax.all_gather(factor_local, 'tile', axis=1, tiled=True)  90.1 us
    gather x2, local copies, waits for them, and re-layouts, contribution(): placed = jnp.take(update, jnp.clip(inverse_map, 0, count - 1), axis=0)  51.4 us
    all_gather x2, waiting for transfers between devices, contribution(): lax.all_gather(inverse_rows, 'tile', axis=0, tiled=True)  43.7 us
    broadcast_in_dim x1, other arithmetic, shards(): return result[None]  23 us
    dot_general x4, matrix products, split_product(): jnp.dot(left_low, right_high, preferred_element_type=jnp.float32)  21 us
    add x2, local copies, waits for them, and re-layouts, split_product(): total + jnp.dot(left_low, right_high, preferred_element_type=jnp.float32)  18.7 us
    dot_general x4, matrix products, split_product(): total = jnp.dot(left_high, right_high, preferred_element_type=jnp.float32)  16.9 us
  transfers between devices with their start and end apart: 9, of which 9 were waited for; matrix products, arithmetic and copies ran while one was open for 21% of the time, Pallas kernels for 0%

commit v1 on v0

v1 whole, which is shorter than its diff:
```python
import functools

import jax
import jax.numpy as jnp
from jax import lax
from jax.experimental import pallas as pl
from jax.experimental.pallas import tpu as pltpu
from jax.sharding import PartitionSpec as P

MESH = pl.DeviceIdType.MESH


def parts(value):
    high = value.astype(jnp.bfloat16)
    return high, (value - high.astype(jnp.float32)).astype(jnp.bfloat16)


def dot(left, right, contract=(1, 0)):
    dims = (((contract[0],), (contract[1],)), ((), ()))
    return lax.dot_general(left, right, dims, preferred_element_type=jnp.float32)


def split_product(left, right):
    total = dot(left[0], right[0])
    total = total + dot(left[0], right[1])
    return total + dot(left[1], right[0])


def update_kernel(
    n, inv_in, up_in, low_in, map_ref, u_out,
    up, inv, low, up_h, up_l, inv_h, inv_l, f_end, f_own, f_h, f_l, stage,
    local_sem, part_send, part_recv, up_send, up_recv, inv_send, inv_recv,
    low_send, low_recv, f_send, f_recv, out_sem,
):
    t = lax.axis_index("tile")
    f = lax.axis_index("front")
    partner = lax.rem(f, 2) * -2 + 1 + f
    count = map_ref.shape[2]
    wc = up.shape[3]
    kr = inv.shape[2]
    width = f_own.shape[2]
    chunk = min(256, width)
    middle = (t >= 1) & (t <= n - 2)
    at_end = (t == 0) | (t == n - 1)

    barrier = pltpu.get_barrier_semaphore()
    pl.semaphore_signal(barrier, inc=1, device_id=(partner, t), device_id_type=MESH)

    @pl.when(t > 0)
    def _():
        pl.semaphore_signal(barrier, inc=1, device_id=(f, t - 1), device_id_type=MESH)

    @pl.when(t < n - 1)
    def _():
        pl.semaphore_signal(barrier, inc=1, device_id=(f, t + 1), device_id_type=MESH)

    @pl.when(at_end)
    def _():
        pl.semaphore_wait(barrier, 2)

    @pl.when(middle)
    def _():
        pl.semaphore_wait(barrier, 3)

    sources = (up_in, inv_in, low_in)
    targets = (up, inv, low)

    def local(kind):
        return pltpu.make_async_copy(sources[kind].at[0], targets[kind].at[0, t], local_sem.at[kind])

    def exchange(kind):
        return pltpu.make_async_remote_copy(
            src_ref=sources[kind].at[1], dst_ref=targets[kind].at[1, t],
            send_sem=part_send.at[kind], recv_sem=part_recv.at[kind],
            device_id=(partner, t), device_id_type=MESH,
        )

    def hop(kind, child, shard, side):
        send, recv = ((up_send, up_recv), (inv_send, inv_recv), (low_send, low_recv))[kind]
        ref = targets[kind].at[child, shard]
        return pltpu.make_async_remote_copy(
            src_ref=ref, dst_ref=ref,
            send_sem=send.at[side, child, shard], recv_sem=recv.at[child, shard],
            device_id=(f, lax.rem(t + (1 if side == 0 else n - 1), n)), device_id_type=MESH,
        )

    def takes(kind, side):
        if kind == 2:
            return t + 1 <= n - 1 if side == 0 else t - 1 >= 0
        return t + 1 <= n - 2 if side == 0 else t - 1 >= 1

    def send(kind, child, shard, side):
        @pl.when(takes(kind, side))
        def _():
            hop(kind, child, shard, side).start()

    def send_own(kind, child):
        send(kind, child, t, 0)
        send(kind, child, t, 1)

    def relay(kinds, child, d):
        for side, shard, valid in ((0, t - d, t - d >= 0), (1, t + d, t + d <= n - 1)):
            @pl.when(valid & (middle if 0 in kinds else t >= 0))
            def _():
                for kind in kinds:
                    hop(kind, child, shard, side).wait_recv()
                    send(kind, child, shard, side)

    def split_child(child):
        @pl.loop(0, n)
        def _(s):
            high, low_part = parts(up[child, s])
            up_h[s] = high
            up_l[s] = low_part
            rows = pl.ds(pl.multiple_of(s * kr, kr), kr)
            high, low_part = parts(inv[child, s])
            inv_h[rows, :] = high
            inv_l[rows, :] = low_part

    def factor(child, start, dst):
        @pl.loop(0, width // chunk)
        def _(j):
            base = pl.multiple_of(j * chunk, chunk)
            columns = lax.broadcasted_iota(jnp.int32, (chunk, wc), 0) + (start + base)
            high = low_part = None
            for s in range(n):
                listed = map_ref[child, :, s * wc:(s + 1) * wc]
                choose = (columns == listed).astype(jnp.float32).astype(jnp.bfloat16)
                a = dot(up_h[s], choose, (1, 1))
                b = dot(up_l[s], choose, (1, 1))
                high = a if high is None else high + a
                low_part = b if low_part is None else low_part + b
            picked = (high.astype(jnp.bfloat16), low_part.astype(jnp.bfloat16))
            dst[child, :, pl.ds(base, chunk)] = split_product((inv_h[...], inv_l[...]), picked)

    def end_copy(child, side):
        return pltpu.make_async_remote_copy(
            src_ref=f_end.at[child], dst_ref=f_own.at[child],
            send_sem=f_send.at[child], recv_sem=f_recv.at[child],
            device_id=(f, lax.rem(t + (1 if side == 0 else n - 1), n)), device_id_type=MESH,
        )

    def serve(child):
        @pl.when(middle)
        def _():
            split_child(child)

            @pl.when(t == n - 2)
            def _():
                factor(child, (n - 1) * width, f_end)
                end_copy(child, 0).start()

            @pl.when(t == 1)
            def _():
                factor(child, 0, f_end)
                end_copy(child, 1).start()

            factor(child, t * width, f_own)

    def split_factor(child):
        @pl.when(at_end)
        def _():
            end_copy(child, 0).wait_recv()

        @pl.loop(0, width // chunk)
        def _(j):
            cols = pl.ds(pl.multiple_of(j * chunk, chunk), chunk)
            high, low_part = parts(f_own[child, :, cols])
            f_h[child, :, cols] = high
            f_l[child, :, cols] = low_part

    def put(child, shard):
        left = parts(low[child, shard])

        @pl.loop(0, width // chunk)
        def _(j):
            cols = pl.ds(pl.multiple_of(j * chunk, chunk), chunk)
            stage[:, cols] = split_product(left, (f_h[child, :, cols], f_l[child, :, cols]))

        copy = pltpu.make_async_copy(stage, u_out.at[child, shard], out_sem)
        copy.start()
        copy.wait()

    for kind in range(3):
        exchange(kind).start()
        local(kind).start()
    for kind in range(3):
        local(kind).wait()
    send_own(0, 0)
    send_own(1, 0)

    @pl.when(t == n - 2)
    def _():
        hop(2, 0, t, 0).start()

    @pl.when(t == 1)
    def _():
        hop(2, 0, t, 1).start()

    for kind in range(3):
        exchange(kind).wait()

    @pl.when(t == n - 2)
    def _():
        hop(2, 1, t, 0).start()

    @pl.when(t == 1)
    def _():
        hop(2, 1, t, 1).start()

    @pl.loop(1, n)
    def _(d):
        relay((0, 1), 0, d)

    send_own(0, 1)
    send_own(1, 1)
    serve(0)

    @pl.loop(1, n)
    def _(d):
        relay((0, 1), 1, d)

    for child in range(2):
        @pl.when((t < n - 1) & (t != n - 2))
        def _():
            hop(2, child, t, 0).start()

        @pl.when((t > 0) & (t != 1))
        def _():
            hop(2, child, t, 1).start()

    serve(1)
    for child in range(2):
        split_factor(child)

    @pl.loop(0, 2)
    def _(child):
        put(child, t)

    @pl.loop(1, n)
    def _(d):
        for child in range(2):
            relay((2,), child, d)

        @pl.loop(0, 2)
        def _(child):
            @pl.when(t - d >= 0)
            def _():
                put(child, t - d)

            @pl.when(t + d <= n - 1)
            def _():
                put(child, t + d)

    for child in range(2):
        @pl.loop(0, n)
        def _(s):
            for side in range(2):
                for kind in range(3):
                    @pl.when(takes(kind, side) & (s <= t if side == 0 else s >= t))
                    def _():
                        hop(kind, child, s, side).wait_send()

        @pl.when((t == n - 2) | (t == 1))
        def _():
            end_copy(child, 0).wait_send()


def gathered_updates(inverse, upper, lower, maps, n, width):
    pivots = inverse.shape[2]
    kr, wc, lr = inverse.shape[1], upper.shape[2], lower.shape[1]
    vmem = pltpu.VMEM
    dma = pltpu.SemaphoreType.DMA
    f32, b16 = jnp.float32, jnp.bfloat16
    return pl.pallas_call(
        functools.partial(update_kernel, n),
        out_shape=jax.ShapeDtypeStruct((2, n, lr, width), f32),
        in_specs=[pl.BlockSpec(memory_space=pl.ANY)] * 3 + [pl.BlockSpec(memory_space=vmem)],
        out_specs=pl.BlockSpec(memory_space=pl.ANY),
        scratch_shapes=[
            vmem((2, n, pivots, wc), f32),
            vmem((2, n, kr, pivots), f32),
            vmem((2, n, lr, pivots), f32),
            vmem((n, pivots, wc), b16),
            vmem((n, pivots, wc), b16),
            vmem((n * kr, pivots), b16),
            vmem((n * kr, pivots), b16),
            vmem((2, pivots, width), f32),
            vmem((2, pivots, width), f32),
            vmem((2, pivots, width), b16),
            vmem((2, pivots, width), b16),
            vmem((lr, width), f32),
            dma((3,)), dma((3,)), dma((3,)),
            dma((2, 2, n)), dma((2, n)),
            dma((2, 2, n)), dma((2, n)),
            dma((2, 2, n)), dma((2, n)),
            dma((2,)), dma((2,)), dma,
        ],
        compiler_params=pltpu.CompilerParams(
            collective_id=0, has_side_effects=True, vmem_limit_bytes=56 * 1024 * 1024
        ),
    )(inverse, upper, lower, maps)


def place_kernel(first_ref, second_ref, base_ref, u_ref, out_ref, u, rows, sem):
    block = base_ref.shape[0]
    total = u_ref.shape[0]
    start = pl.program_id(0) * block

    @pl.when(pl.program_id(0) == 0)
    def _():
        copy = pltpu.make_async_copy(u_ref, u.at[pl.ds(0, total)], sem)
        copy.start()
        u[pl.ds(total, 8), :] = jnp.zeros((8, u.shape[1]), jnp.float32)
        copy.wait()

    @pl.loop(0, block // 8)
    def _(i):
        for j in range(8):
            r = i * 8 + j
            a = u[pl.ds(first_ref[start + r], 1), :]
            b = u[pl.ds(second_ref[start + r], 1), :]
            rows[pl.ds(r, 1), :] = a + b

    out_ref[...] = base_ref[...] - rows[...]


def placed(base, updates, first, second):
    order, width = base.shape
    block = 256
    return pl.pallas_call(
        place_kernel,
        out_shape=jax.ShapeDtypeStruct(base.shape, base.dtype),
        grid_spec=pltpu.PrefetchScalarGridSpec(
            num_scalar_prefetch=2,
            grid=(order // block,),
            in_specs=[
                pl.BlockSpec((block, width), lambda i, *_: (i, 0)),
                pl.BlockSpec(memory_space=pl.ANY),
            ],
            out_specs=pl.BlockSpec((block, width), lambda i, *_: (i, 0)),
            scratch_shapes=[
                pltpu.VMEM((updates.shape[0] + 8, width), jnp.float32),
                pltpu.VMEM((block, width), jnp.float32),
                pltpu.SemaphoreType.DMA,
            ],
        ),
        compiler_params=pltpu.CompilerParams(vmem_limit_bytes=40 * 1024 * 1024),
    )(first, second, base, updates)


def shards(pivot_inverse, panel_upper, panel_lower, index_map, parent_base):
    base = parent_base[0]
    order, width = base.shape
    n = lax.axis_size("tile")
    group = lax.axis_index("front")
    partner = jnp.bitwise_xor(group, 1)
    count = index_map.shape[2]
    maps = jnp.stack([
        lax.dynamic_index_in_dim(index_map, group, 0, keepdims=False)[0],
        lax.dynamic_index_in_dim(index_map, partner, 0, keepdims=False)[1],
    ])
    updates = gathered_updates(
        pivot_inverse[0], panel_upper[0], panel_lower[0], maps[:, None, :], n, width
    )
    rows = jnp.arange(order, dtype=jnp.int32)
    listed = jnp.arange(count, dtype=jnp.int32)
    sources = []
    for child in range(2):
        hit = maps[child][None, :] == rows[:, None]
        place = jnp.max(jnp.where(hit, listed[None, :], -1), axis=1)
        sources.append(jnp.where(place >= 0, place + child * count, 2 * count))
    return placed(base, updates.reshape(2 * count, width), sources[0], sources[1])[None]


def solution(mesh):
    return jax.shard_map(
        shards,
        mesh=mesh,
        in_specs=(
            P("front", None, "tile", None),
            P("front", None, None, "tile"),
            P("front", None, "tile", None),
            P(),
            P("front", None, "tile"),
        ),
        out_specs=P("front", None, "tile"),
        check_vma=False,
    )
```

time: 490 us -> 320 us (0.65)
  Pallas kernels: 0 us -> 309 us
  waiting for transfers between devices: 277 us -> 0 us
  local copies, waits for them, and re-layouts: 117 us -> 1.37 us
  matrix products: 44.7 us -> 0 us
  other arithmetic: 36.1 us -> 9.02 us
  between operations: 13.7 us -> 0.21 us
    pallas_call x0 -> x2, Pallas kernels: none -> 309 us  [the longest x1 272 us: gathered_updates(): pl.pallas_call(functools.partial(update_kernel, n), out_shape=jax.ShapeDt...]
    all_gather x6 -> x0, waiting for transfers between devices: 270 us -> none  [the longest x2 136 us: contribution(): lax.all_gather(lower_rows, 'tile', axis=0, tiled=True)]
    gather x4 -> x0, local copies, waits for them, and re-layouts: 64.2 us -> none  [the longest x2 51.4 us: contribution(): placed = jnp.take(update, jnp.clip(inverse_map, 0, count - 1), axis=0)]
    dot_general x12 -> x0, matrix products: 44.7 us -> none  [the longest x4 21 us: split_product(): jnp.dot(left_low, right_high, preferred_element_type=jnp.float32)]
    broadcast_in_dim x1 -> x0, other arithmetic: 23 us -> none  [shards(): return result[None]]
    add x2 -> x0, local copies, waits for them, and re-layouts: 18.7 us -> none  [split_product(): total + jnp.dot(left_low, right_high, preferred_element_type=jnp.float32)]
    scatter x2 -> x0, local copies, waits for them, and re-layouts: 16.3 us -> none  [contribution(): jnp.full((parent_order,), -1, jnp.int32).at[mapping]]
    convert_element_type x7 -> x0, other arithmetic: 12.2 us -> none  [split_parts(): high = matrix.astype(jnp.bfloat16)]
  transfers between devices with their start and end apart: 9 -> 0, of which waited for: 9 -> 0; matrix products, arithmetic and copies ran while one was open for 21% -> 0% of each run, Pallas kernels for 0% -> 0%
where the time goes in v1:
time: 320 us
  Pallas kernels  309 us (97%)
  other arithmetic  9.02 us (3%)
    pallas_call x1, Pallas kernels, gathered_updates(): pl.pallas_call(functools.partial(update_kernel, n), out_shape=jax.ShapeDt...  272 us
    pallas_call x1, Pallas kernels, placed(): pl.pallas_call(place_kernel, out_shape=jax.ShapeDtypeStruct(base.shape, b...  37.7 us
    reduce_max x2, other arithmetic, shards(): place = jnp.max(jnp.where(hit, listed[None, :], -1), axis=1)  9 us

profile of v1, /device:TPU:0, one launch (start us, length us, event | category | flops | bytes accessed | tf_op | source)
XLA Modules:
  0.0 319.9 jit_solution(11494275481670104866)
XLA Ops:
  0.0 0.7 constant_dynamic-slice_fusion
  0.8 4.5 %select_reduce_fusion.1 = s32[4096]{0:T(1024)S(1)} fusion(s32[2048]{0:T(1024)S(1)} %bitcast.17), kind=kLoop, calls=%fused_computation.2 | loop fusion | flops 25161728 | bytes 24576 | tf_op jit(solution)/shard_map/reduce_max | solution.py:371
  5.3 0.6 broadcast_in_dim.37.map_ref
  5.9 4.5 %select_reduce_fusion = s32[4096]{0:T(1024)S(1)} fusion(s32[2048]{0:T(1024)S(1)} %bitcast.16), kind=kLoop, calls=%fused_computation | loop fusion | flops 25161728 | bytes 24576 | tf_op jit(solution)/shard_map/reduce_max | solution.py:371
  10.4 271.6 %shard_map.55 = f32[2,4,512,1024]{3,2,1,0:T(8,128)} custom-call(f32[2,128,512]{2,1,0:T(8,128)} %bitcast.14, f32[2,512,512]{2,1,0:T(8,128)} %bitcast.12, f32[2,512,512]{2,1,0:T(8,128)} %bitcast.13, s32[2,1,2048]{2,1,0:T(1,128)} %broadcast_in_dim.37.map_ref), custom_call_target="tpu_custom_call" | custom-call | tf_op jit(solution)/shard_map/pallas_call | solution.py:275
  282.0 37.7 %shard_map.56 = f32[4096,1024]{1,0:T(8,128)} custom-call(s32[4096]{0:T(1024)S(1)} %get-tuple-element.7.first_ref, s32[4096]{0:T(1024)S(1)} %get-tuple-element.8.second_ref, f32[4096,1024]{1,0:T(8,128)} %bitcast.11, f32[4096,1024]{1,0:T(8,128)} %bitcast.10), custom_call_target="tpu_custom_call" | custom-call | tf_op jit(solution)/shard_map/pallas_call | solution.py:331
  (2 shorter events, 0.0 us)

commit v2 on v1

--- a/solution.py
+++ b/solution.py
@@ -27,7 +27,7 @@
 
 
 def update_kernel(
-    n, inv_in, up_in, low_in, map_ref, u_out,
+    n, inv_in, up_in, low_in, map_ref, u_out, index_out,
     up, inv, low, up_h, up_l, inv_h, inv_l, f_end, f_own, f_h, f_l, stage,
     local_sem, part_send, part_recv, up_send, up_recv, inv_send, inv_recv,
     low_send, low_recv, f_send, f_recv, out_sem,
@@ -117,7 +117,7 @@
             inv_h[rows, :] = high
             inv_l[rows, :] = low_part
 
-    def factor(child, start, dst):
+    def factor(child, start, dst, after):
         @pl.loop(0, width // chunk)
         def _(j):
             base = pl.multiple_of(j * chunk, chunk)
@@ -132,35 +132,37 @@
                 low_part = b if low_part is None else low_part + b
             picked = (high.astype(jnp.bfloat16), low_part.astype(jnp.bfloat16))
             dst[child, :, pl.ds(base, chunk)] = split_product((inv_h[...], inv_l[...]), picked)
-
-    def end_copy(child, side):
+            after(j)
+
+    def end_copy(child, j, target):
+        cols = pl.ds(pl.multiple_of(j * chunk, chunk), chunk)
         return pltpu.make_async_remote_copy(
-            src_ref=f_end.at[child], dst_ref=f_own.at[child],
-            send_sem=f_send.at[child], recv_sem=f_recv.at[child],
-            device_id=(f, lax.rem(t + (1 if side == 0 else n - 1), n)), device_id_type=MESH,
+            src_ref=f_end.at[child, :, cols], dst_ref=f_own.at[child, :, cols],
+            send_sem=f_send.at[child, j], recv_sem=f_recv.at[child, j],
+            device_id=(f, target), device_id_type=MESH,
         )
+
+    server = (t == 1) | (t == n - 2)
+    end = lax.div(t - 1, n - 3) * (n - 1)
+    aside = lax.rem(t + 1, n)
 
     def serve(child):
         @pl.when(middle)
         def _():
             split_child(child)
 
-            @pl.when(t == n - 2)
+            @pl.when(server)
             def _():
-                factor(child, (n - 1) * width, f_end)
-                end_copy(child, 0).start()
-
-            @pl.when(t == 1)
-            def _():
-                factor(child, 0, f_end)
-                end_copy(child, 1).start()
-
-            factor(child, t * width, f_own)
+                factor(child, end * width, f_end, lambda j: end_copy(child, j, end).start())
+
+            factor(child, t * width, f_own, lambda j: None)
 
     def split_factor(child):
         @pl.when(at_end)
         def _():
-            end_copy(child, 0).wait_recv()
+            @pl.loop(0, width // chunk)
+            def _(j):
+                end_copy(child, j, aside).wait_recv()
 
         @pl.loop(0, width // chunk)
         def _(j):
@@ -169,17 +171,40 @@
             f_h[child, :, cols] = high
             f_l[child, :, cols] = low_part
 
+    lr = low.shape[2]
+    tall = stage.shape[0] // lr
+
     def put(child, shard):
         left = parts(low[child, shard])
 
         @pl.loop(0, width // chunk)
         def _(j):
             cols = pl.ds(pl.multiple_of(j * chunk, chunk), chunk)
-            stage[:, cols] = split_product(left, (f_h[child, :, cols], f_l[child, :, cols]))
+            block = split_product(left, (f_h[child, :, cols], f_l[child, :, cols]))
+            for q in range(chunk // 128):
+                strip = pl.ds(j * (chunk // 128) + q, lr, stride=tall)
+                stage[strip, :] = block[:, q * 128:(q + 1) * 128]
 
         copy = pltpu.make_async_copy(stage, u_out.at[child, shard], out_sem)
         copy.start()
         copy.wait()
+
+    def index_rows():
+        shape = (8, count)
+        place = lax.broadcasted_iota(jnp.int32, shape, 1)
+        which = lax.broadcasted_iota(jnp.int32, shape, 0)
+        digits = jnp.where(which == 0, place >> 7, jnp.where(which == 1, place & 127, 1))
+        digits = digits.astype(jnp.float32).astype(jnp.bfloat16)
+        span = min(256, index_out.shape[2])
+        for child in range(2):
+            @pl.loop(0, index_out.shape[2] // span)
+            def _(j):
+                base = pl.multiple_of(j * span, span)
+                rows = lax.broadcasted_iota(jnp.int32, (span, count), 0) + base
+                choose = (rows == map_ref[child]).astype(jnp.float32).astype(jnp.bfloat16)
+                found = dot(digits, choose, (1, 1)).astype(jnp.int32)
+                source = found[0:1] * 128 + found[1:2] + child * count
+                index_out[child, :, pl.ds(base, span)] = jnp.where(found[2:3] > 0, source, 2 * count)
 
     for kind in range(3):
         exchange(kind).start()
@@ -208,6 +233,8 @@
     def _():
         hop(2, 1, t, 1).start()
 
+    index_rows()
+
     @pl.loop(1, n)
     def _(d):
         relay((0, 1), 0, d)
@@ -239,11 +266,10 @@
 
     @pl.loop(1, n)
     def _(d):
-        for child in range(2):
-            relay((2,), child, d)
-
         @pl.loop(0, 2)
         def _(child):
+            relay((2,), child, d)
+
             @pl.when(t - d >= 0)
             def _():
                 put(child, t - d)
@@ -261,22 +287,29 @@
                     def _():
                         hop(kind, child, s, side).wait_send()
 
-        @pl.when((t == n - 2) | (t == 1))
-        def _():
-            end_copy(child, 0).wait_send()
-
-
-def gathered_updates(inverse, upper, lower, maps, n, width):
+        @pl.when(server)
+        def _():
+            @pl.loop(0, width // chunk)
+            def _(j):
+                end_copy(child, j, aside).wait_send()
+
+
+def gathered_updates(inverse, upper, lower, maps, n, order, width):
     pivots = inverse.shape[2]
     kr, wc, lr = inverse.shape[1], upper.shape[2], lower.shape[1]
     vmem = pltpu.VMEM
     dma = pltpu.SemaphoreType.DMA
     f32, b16 = jnp.float32, jnp.bfloat16
+    chunks = width // min(256, width)
+    tall = -(-width // 1024) * 8
     return pl.pallas_call(
         functools.partial(update_kernel, n),
-        out_shape=jax.ShapeDtypeStruct((2, n, lr, width), f32),
+        out_shape=(
+            jax.ShapeDtypeStruct((2, n, lr * tall, 128), f32),
+            jax.ShapeDtypeStruct((2, 1, order), jnp.int32),
+        ),
         in_specs=[pl.BlockSpec(memory_space=pl.ANY)] * 3 + [pl.BlockSpec(memory_space=vmem)],
-        out_specs=pl.BlockSpec(memory_space=pl.ANY),
+        out_specs=(pl.BlockSpec(memory_space=pl.ANY), pl.BlockSpec(memory_space=vmem)),
         scratch_shapes=[
             vmem((2, n, pivots, wc), f32),
             vmem((2, n, kr, pivots), f32),
@@ -289,12 +322,12 @@
             vmem((2, pivots, width), f32),
             vmem((2, pivots, width), b16),
             vmem((2, pivots, width), b16),
-            vmem((lr, width), f32),
+            vmem((lr * tall, 128), f32),
             dma((3,)), dma((3,)), dma((3,)),
             dma((2, 2, n)), dma((2, n)),
             dma((2, 2, n)), dma((2, n)),
             dma((2, 2, n)), dma((2, n)),
-            dma((2,)), dma((2,)), dma,
+            dma((2, chunks)), dma((2, chunks)), dma,
         ],
         compiler_params=pltpu.CompilerParams(
             collective_id=0, has_side_effects=True, vmem_limit_bytes=56 * 1024 * 1024
@@ -302,37 +335,42 @@
     )(inverse, upper, lower, maps)
 
 
-def place_kernel(first_ref, second_ref, base_ref, u_ref, out_ref, u, rows, sem):
-    block = base_ref.shape[0]
+def place_kernel(index_ref, base_ref, u_ref, out_ref, u, rows, sem):
+    block, width = base_ref.shape
+    order = block * pl.num_programs(0)
     total = u_ref.shape[0]
+    tall = rows.shape[0] // block
     start = pl.program_id(0) * block
 
     @pl.when(pl.program_id(0) == 0)
     def _():
         copy = pltpu.make_async_copy(u_ref, u.at[pl.ds(0, total)], sem)
         copy.start()
-        u[pl.ds(total, 8), :] = jnp.zeros((8, u.shape[1]), jnp.float32)
+        u[pl.ds(total, tall), :] = jnp.zeros((tall, 128), jnp.float32)
         copy.wait()
 
     @pl.loop(0, block // 8)
     def _(i):
         for j in range(8):
             r = i * 8 + j
-            a = u[pl.ds(first_ref[start + r], 1), :]
-            b = u[pl.ds(second_ref[start + r], 1), :]
-            rows[pl.ds(r, 1), :] = a + b
-
-    out_ref[...] = base_ref[...] - rows[...]
-
-
-def placed(base, updates, first, second):
+            a = u[pl.ds(pl.multiple_of(index_ref[start + r] * tall, tall), tall), :]
+            b = u[pl.ds(pl.multiple_of(index_ref[order + start + r] * tall, tall), tall), :]
+            rows[pl.ds(pl.multiple_of(r * tall, tall), tall), :] = a + b
+
+    for q in range(width // 128):
+        cols = slice(q * 128, (q + 1) * 128)
+        out_ref[:, cols] = base_ref[:, cols] - rows[pl.ds(q, block, stride=tall), :]
+
+
+def placed(base, updates, index):
     order, width = base.shape
-    block = 256
+    block = min(256, order)
+    tall = -(-width // 1024) * 8
     return pl.pallas_call(
         place_kernel,
         out_shape=jax.ShapeDtypeStruct(base.shape, base.dtype),
         grid_spec=pltpu.PrefetchScalarGridSpec(
-            num_scalar_prefetch=2,
+            num_scalar_prefetch=1,
             grid=(order // block,),
             in_specs=[
                 pl.BlockSpec((block, width), lambda i, *_: (i, 0)),
@@ -340,13 +378,13 @@
             ],
             out_specs=pl.BlockSpec((block, width), lambda i, *_: (i, 0)),
             scratch_shapes=[
-                pltpu.VMEM((updates.shape[0] + 8, width), jnp.float32),
-                pltpu.VMEM((block, width), jnp.float32),
+                pltpu.VMEM((updates.shape[0] + tall, 128), jnp.float32),
+                pltpu.VMEM((block * tall, 128), jnp.float32),
                 pltpu.SemaphoreType.DMA,
             ],
         ),
         compiler_params=pltpu.CompilerParams(vmem_limit_bytes=40 * 1024 * 1024),
-    )(first, second, base, updates)
+    )(index, base, updates)
 
 
 def shards(pivot_inverse, panel_upper, panel_lower, index_map, parent_base):
@@ -355,22 +393,14 @@
     n = lax.axis_size("tile")
     group = lax.axis_index("front")
     partner = jnp.bitwise_xor(group, 1)
-    count = index_map.shape[2]
     maps = jnp.stack([
         lax.dynamic_index_in_dim(index_map, group, 0, keepdims=False)[0],
         lax.dynamic_index_in_dim(index_map, partner, 0, keepdims=False)[1],
     ])
-    updates = gathered_updates(
-        pivot_inverse[0], panel_upper[0], panel_lower[0], maps[:, None, :], n, width
+    updates, index = gathered_updates(
+        pivot_inverse[0], panel_upper[0], panel_lower[0], maps[:, None, :], n, order, width
     )
-    rows = jnp.arange(order, dtype=jnp.int32)
-    listed = jnp.arange(count, dtype=jnp.int32)
-    sources = []
-    for child in range(2):
-        hit = maps[child][None, :] == rows[:, None]
-        place = jnp.max(jnp.where(hit, listed[None, :], -1), axis=1)
-        sources.append(jnp.where(place >= 0, place + child * count, 2 * count))
-    return placed(base, updates.reshape(2 * count, width), sources[0], sources[1])[None]
+    return placed(base, updates.reshape(-1, 128), index.reshape(-1))[None]
 
 
 def solution(mesh):

time: 320 us -> 294 us (0.919)
  Pallas kernels: 309 us -> 291 us
  other arithmetic: 9.02 us -> 0.02 us
    pallas_call x1, Pallas kernels: 272 us -> 261 us  [gathered_updates(): pl.pallas_call(functools.partial(update_kernel, n), out_shape=(jax.ShapeD...]
    reduce_max x2 -> x0, other arithmetic: 9 us -> none  [shards(): place = jnp.max(jnp.where(hit, listed[None, :], -1), axis=1)]
    pallas_call x1, Pallas kernels: 37.7 us -> 30.5 us  [placed(): pl.pallas_call(place_kernel, out_shape=jax.ShapeDtypeStruct(base.shape, b...]
where the time goes in v2:
time: 294 us
  Pallas kernels  291 us (99%)
    pallas_call x1, Pallas kernels, gathered_updates(): pl.pallas_call(functools.partial(update_kernel, n), out_shape=(jax.ShapeD...  261 us
    pallas_call x1, Pallas kernels, placed(): pl.pallas_call(place_kernel, out_shape=jax.ShapeDtypeStruct(base.shape, b...  30.5 us

profile of v2, /device:TPU:0, one launch (start us, length us, event | category | flops | bytes accessed | tf_op | source)
XLA Modules:
  0.0 293.5 jit_solution(17594648726287717728)
XLA Ops:
  0.0 0.8 dynamic-slice_bitcast_fusion.1
  0.8 0.6 broadcast_in_dim.6.map_ref
  1.4 260.8 %shard_map.55 = (f32[2,4,4096,128]{3,2,1,0:T(8,128)}, s32[2,1,4096]{2,1,0:T(1,128)}) custom-call(f32[2,128,512]{2,1,0:T(8,128)} %bitcast.16, f32[2,512,512]{2,1,0:T(8,128)} %bitcast.14, f32[2,512,512]{2,1,0:T(8,128)} %bitcast.15, s32[2,1,2048]{2,1,0:T(1,128)} %broadcast_in_dim.6.map_ref), custom_call_target="tpu_custom_call" | custom-call | tf_op jit(solution)/shard_map/pallas_call | solution.py:305
  262.2 0.0 copy-start
  262.2 0.7 copy-done
  263.0 30.5 %shard_map.56 = f32[4096,1024]{1,0:T(8,128)} custom-call(s32[8192]{0:T(1024)S(1)} %bitcast.11, f32[4096,1024]{1,0:T(8,128)} %bitcast.12, f32[32768,128]{1,0:T(8,128)} %bitcast.13), custom_call_target="tpu_custom_call" | custom-call | tf_op jit(solution)/shard_map/pallas_call | solution.py:369
  (1 shorter events, 0.0 us)
Async XLA Ops:
  262.2 0.8 copy-start

commit v3 on v2

--- a/solution.py
+++ b/solution.py
@@ -110,12 +110,12 @@
         @pl.loop(0, n)
         def _(s):
             high, low_part = parts(up[child, s])
-            up_h[s] = high
-            up_l[s] = low_part
+            up_h[child, s] = high
+            up_l[child, s] = low_part
             rows = pl.ds(pl.multiple_of(s * kr, kr), kr)
             high, low_part = parts(inv[child, s])
-            inv_h[rows, :] = high
-            inv_l[rows, :] = low_part
+            inv_h[child, rows, :] = high
+            inv_l[child, rows, :] = low_part
 
     def factor(child, start, dst, after):
         @pl.loop(0, width // chunk)
@@ -126,12 +126,12 @@
             for s in range(n):
                 listed = map_ref[child, :, s * wc:(s + 1) * wc]
                 choose = (columns == listed).astype(jnp.float32).astype(jnp.bfloat16)
-                a = dot(up_h[s], choose, (1, 1))
-                b = dot(up_l[s], choose, (1, 1))
+                a = dot(up_h[child, s], choose, (1, 1))
+                b = dot(up_l[child, s], choose, (1, 1))
                 high = a if high is None else high + a
                 low_part = b if low_part is None else low_part + b
             picked = (high.astype(jnp.bfloat16), low_part.astype(jnp.bfloat16))
-            dst[child, :, pl.ds(base, chunk)] = split_product((inv_h[...], inv_l[...]), picked)
+            dst[child, :, pl.ds(base, chunk)] = split_product((inv_h[child], inv_l[child]), picked)
             after(j)
 
     def end_copy(child, j, target):
@@ -146,7 +146,7 @@
     end = lax.div(t - 1, n - 3) * (n - 1)
     aside = lax.rem(t + 1, n)
 
-    def serve(child):
+    def prepare(child):
         @pl.when(middle)
         def _():
             split_child(child)
@@ -155,6 +155,9 @@
             def _():
                 factor(child, end * width, f_end, lambda j: end_copy(child, j, end).start())
 
+    def own(child):
+        @pl.when(middle)
+        def _():
             factor(child, t * width, f_own, lambda j: None)
 
     def split_factor(child):
@@ -204,7 +207,7 @@
                 choose = (rows == map_ref[child]).astype(jnp.float32).astype(jnp.bfloat16)
                 found = dot(digits, choose, (1, 1)).astype(jnp.int32)
                 source = found[0:1] * 128 + found[1:2] + child * count
-                index_out[child, :, pl.ds(base, span)] = jnp.where(found[2:3] > 0, source, 2 * count)
+                index_out[child, :, pl.ds(base, span)] = jnp.where(found[2:3] > 0, source, 2 * count) * tall
 
     for kind in range(3):
         exchange(kind).start()
@@ -233,30 +236,35 @@
     def _():
         hop(2, 1, t, 1).start()
 
+    relay((0, 1), 0, 1)
+    send_own(0, 1)
+    send_own(1, 1)
     index_rows()
 
-    @pl.loop(1, n)
+    @pl.loop(2, n)
     def _(d):
         relay((0, 1), 0, d)
 
-    send_own(0, 1)
-    send_own(1, 1)
-    serve(0)
-
-    @pl.loop(1, n)
+    prepare(0)
+    relay((0, 1), 1, 1)
+
+    for child in range(2):
+        @pl.when((t < n - 1) & (t != n - 2))
+        def _():
+            hop(2, child, t, 0).start()
+
+        @pl.when((t > 0) & (t != 1))
+        def _():
+            hop(2, child, t, 1).start()
+
+    own(0)
+
+    @pl.loop(2, n)
     def _(d):
         relay((0, 1), 1, d)
 
-    for child in range(2):
-        @pl.when((t < n - 1) & (t != n - 2))
-        def _():
-            hop(2, child, t, 0).start()
-
-        @pl.when((t > 0) & (t != 1))
-        def _():
-            hop(2, child, t, 1).start()
-
-    serve(1)
+    prepare(1)
+    own(1)
     for child in range(2):
         split_factor(child)
 
@@ -314,10 +322,10 @@
             vmem((2, n, pivots, wc), f32),
             vmem((2, n, kr, pivots), f32),
             vmem((2, n, lr, pivots), f32),
-            vmem((n, pivots, wc), b16),
-            vmem((n, pivots, wc), b16),
-            vmem((n * kr, pivots), b16),
-            vmem((n * kr, pivots), b16),
+            vmem((2, n, pivots, wc), b16),
+            vmem((2, n, pivots, wc), b16),
+            vmem((2, n * kr, pivots), b16),
+            vmem((2, n * kr, pivots), b16),
             vmem((2, pivots, width), f32),
             vmem((2, pivots, width), f32),
             vmem((2, pivots, width), b16),
@@ -349,12 +357,14 @@
         u[pl.ds(total, tall), :] = jnp.zeros((tall, 128), jnp.float32)
         copy.wait()
 
-    @pl.loop(0, block // 8)
+    turn = 32
+
+    @pl.loop(0, block // turn)
     def _(i):
-        for j in range(8):
-            r = i * 8 + j
-            a = u[pl.ds(pl.multiple_of(index_ref[start + r] * tall, tall), tall), :]
-            b = u[pl.ds(pl.multiple_of(index_ref[order + start + r] * tall, tall), tall), :]
+        for j in range(turn):
+            r = i * turn + j
+            a = u[pl.ds(pl.multiple_of(index_ref[start + r], tall), tall), :]
+            b = u[pl.ds(pl.multiple_of(index_ref[order + start + r], tall), tall), :]
             rows[pl.ds(pl.multiple_of(r * tall, tall), tall), :] = a + b
 
     for q in range(width // 128):

time: 294 us -> 294 us (level)
  no operation moved by 1% of the time
where the time goes in v3:
time: 294 us
  Pallas kernels  291 us (99%)
    pallas_call x1, Pallas kernels, gathered_updates(): pl.pallas_call(functools.partial(update_kernel, n), out_shape=(jax.ShapeD...  263 us
    pallas_call x1, Pallas kernels, placed(): pl.pallas_call(place_kernel, out_shape=jax.ShapeDtypeStruct(base.shape, b...  28.4 us

profile of v3, /device:TPU:0, one launch (start us, length us, event | category | flops | bytes accessed | tf_op | source)
XLA Modules:
  0.0 293.6 jit_solution(10299510426351176693)
XLA Ops:
  0.0 0.8 dynamic-slice_bitcast_fusion.1
  0.8 0.6 broadcast_in_dim.6.map_ref
  1.4 263.1 %shard_map.55 = (f32[2,4,4096,128]{3,2,1,0:T(8,128)}, s32[2,1,4096]{2,1,0:T(1,128)}) custom-call(f32[2,128,512]{2,1,0:T(8,128)} %bitcast.16, f32[2,512,512]{2,1,0:T(8,128)} %bitcast.14, f32[2,512,512]{2,1,0:T(8,128)} %bitcast.15, s32[2,1,2048]{2,1,0:T(1,128)} %broadcast_in_dim.6.map_ref), custom_call_target="tpu_custom_call" | custom-call | tf_op jit(solution)/shard_map/pallas_call | solution.py:313
  264.5 0.0 copy-start
  264.5 0.7 copy-done
  265.2 28.4 %shard_map.56 = f32[4096,1024]{1,0:T(8,128)} custom-call(s32[8192]{0:T(1024)S(1)} %bitcast.11, f32[4096,1024]{1,0:T(8,128)} %bitcast.12, f32[32768,128]{1,0:T(8,128)} %bitcast.13), custom_call_target="tpu_custom_call" | custom-call | tf_op jit(solution)/shard_map/pallas_call | solution.py:379
  (1 shorter events, 0.0 us)
Async XLA Ops:
  264.5 0.8 copy-start

commit v4 on v2

--- a/solution.py
+++ b/solution.py
@@ -349,10 +349,12 @@
         u[pl.ds(total, tall), :] = jnp.zeros((tall, 128), jnp.float32)
         copy.wait()
 
-    @pl.loop(0, block // 8)
+    turn = 32
+
+    @pl.loop(0, block // turn)
     def _(i):
-        for j in range(8):
-            r = i * 8 + j
+        for j in range(turn):
+            r = i * turn + j
             a = u[pl.ds(pl.multiple_of(index_ref[start + r] * tall, tall), tall), :]
             b = u[pl.ds(pl.multiple_of(index_ref[order + start + r] * tall, tall), tall), :]
             rows[pl.ds(pl.multiple_of(r * tall, tall), tall), :] = a + b

time: 294 us -> 293 us (level)
  no operation moved by 1% of the time
where the time goes in v4:
time: 293 us; the launch traced here: 292 us
  Pallas kernels  290 us (99%)
    pallas_call x1, Pallas kernels, gathered_updates(): pl.pallas_call(functools.partial(update_kernel, n), out_shape=(jax.ShapeD...  261 us
    pallas_call x1, Pallas kernels, placed(): pl.pallas_call(place_kernel, out_shape=jax.ShapeDtypeStruct(base.shape, b...  29.5 us

profile of v4, /device:TPU:0, one launch (start us, length us, event | category | flops | bytes accessed | tf_op | source)
XLA Modules:
  0.0 292.5 jit_solution(14982202948252297826)
XLA Ops:
  0.0 0.8 dynamic-slice_bitcast_fusion.1
  0.8 0.6 broadcast_in_dim.6.map_ref
  1.4 260.8 %shard_map.55 = (f32[2,4,4096,128]{3,2,1,0:T(8,128)}, s32[2,1,4096]{2,1,0:T(1,128)}) custom-call(f32[2,128,512]{2,1,0:T(8,128)} %bitcast.16, f32[2,512,512]{2,1,0:T(8,128)} %bitcast.14, f32[2,512,512]{2,1,0:T(8,128)} %bitcast.15, s32[2,1,2048]{2,1,0:T(1,128)} %broadcast_in_dim.6.map_ref), custom_call_target="tpu_custom_call" | custom-call | tf_op jit(solution)/shard_map/pallas_call | solution.py:305
  262.2 0.0 copy-start
  262.2 0.7 copy-done
  263.0 29.5 %shard_map.56 = f32[4096,1024]{1,0:T(8,128)} custom-call(s32[8192]{0:T(1024)S(1)} %bitcast.11, f32[4096,1024]{1,0:T(8,128)} %bitcast.12, f32[32768,128]{1,0:T(8,128)} %bitcast.13), custom_call_target="tpu_custom_call" | custom-call | tf_op jit(solution)/shard_map/pallas_call | solution.py:371
  (1 shorter events, 0.0 us)
Async XLA Ops:
  262.2 0.8 copy-start
